TPU v7x, 32 devices: a whole 2x2x4 slice. The times are simulated.
32 devices in a mesh: section: 2 (over core), fsdp: 8 (over z, y), tensor: 2 (over x).
Axes of the slice: x: 2, y: 2, z: 4, core: 2. Of those that a mesh axis runs over, the one named last changes fastest.
Arguments:
- inputs: bfloat16 [2, 1024, 1024], P(None, 'fsdp'), may hold values from -6 to 6
- cotangent: float32 [2, 2, 1024, 1024], P('section', None, 'fsdp'), may hold values from -8 to 8
- norm_gains: bfloat16 [2, 2, 1024], P('section', None, 'fsdp'), may hold values from 0.5 to 1.5
- norm_biases: bfloat16 [2, 2, 1024], P('section', None, 'fsdp'), may hold values from -1.796875 to 1.796875
- w_qkv: bfloat16 [2, 1024, 3, 1024], P('section', 'fsdp', None, 'tensor'), may hold values from -0.1875 to 0.1875
- w_out: bfloat16 [2, 1024, 1024], P('section', 'tensor', 'fsdp'), may hold values from -0.75 to 0.75
- w_up: bfloat16 [2, 1024, 4096], P('section', 'fsdp', 'tensor'), may hold values from -0.1875 to 0.1875
- w_down: bfloat16 [2, 4096, 1024], P('section', 'tensor', 'fsdp'), may hold values from -0.09375 to 0.09375
Outputs:
- section_out: bfloat16 [2, 2, 1024, 1024], P('section', None, 'fsdp')
- input_grads: float32 [2, 2, 1024, 1024], P('section', None, 'fsdp')
- gain_grads: float32 [2, 2, 1024], P('section', None, 'fsdp')
- bias_grads: float32 [2, 2, 1024], P('section', None, 'fsdp')
- qkv_grads: float32 [2, 1024, 3, 1024], P('section', 'fsdp', None, 'tensor')
- out_grads: float32 [2, 1024, 1024], P('section', 'tensor', 'fsdp')
- up_grads: float32 [2, 1024, 4096], P('section', 'fsdp', 'tensor')
- down_grads: float32 [2, 4096, 1024], P('section', 'tensor', 'fsdp')
All inputs are finite; a program needn't handle non-finite values.
Results may differ from a plain program's by a relative error of at most 0.014.
Values may be sent and summed in bfloat16 or wider, within the bound.
A program may use at most 128 MiB of HBM per device.

v0:
```python
import math
import jax
import jax.numpy as jnp
from jax import lax
from jax.sharding import PartitionSpec as P

HD = 64
SEQ = 128
EPS = 1e-05


def shifted(x, axis, by):
    peers = lax.axis_size(axis)
    pairs = [(i, i + by) for i in range(peers) if 0 <= i + by < peers]
    return lax.ppermute(x, axis, pairs)


def angles(positions, head_dim):
    rot = head_dim // 4
    half = rot // 2
    freq = 10000.0 ** (-(jnp.arange(half).astype(jnp.float32) * 2.0 / rot))
    theta = positions.astype(jnp.float32)[:, None] * freq[None, :]
    return (jnp.cos(theta), jnp.sin(theta))


def rotate(value, cosine, sine):
    half = cosine.shape[1]
    first = value[..., :half]
    second = value[..., half : 2 * half]
    rest = value[..., 2 * half :]
    cpart = cosine[:, None, :]
    spart = sine[:, None, :]
    return jnp.concatenate(
        [first * cpart - second * spart, second * cpart + first * spart, rest], axis=-1
    )


def normalize(u):
    whole = u.astype(jnp.float32)
    centred = whole - jnp.mean(whole, axis=-1, keepdims=True)
    rstd = lax.rsqrt(jnp.mean(centred * centred, axis=-1, keepdims=True) + EPS)
    return (centred * rstd, rstd)


def gelu_slope(hidden):
    return 0.5 * (1.0 + lax.erf(hidden / math.sqrt(2.0))) + hidden * jnp.exp(
        -0.5 * hidden * hidden
    ) / math.sqrt(2.0 * math.pi)


def grouped(value):
    return value.reshape((value.shape[0] // SEQ, SEQ) + value.shape[1:])


def masked_scores(query, key):
    scores = jnp.einsum("sqhd,skhd->shqk", query, key, preferred_element_type=jnp.float32)
    places = jnp.arange(SEQ, dtype=jnp.int32)
    return jnp.where(places[None, :] <= places[:, None], scores, -1e30)


def attention_forward(query, key, value):
    tokens, heads = (query.shape[0], query.shape[1])
    scores = masked_scores(grouped(query), grouped(key))
    top = jnp.max(scores, axis=-1, keepdims=True)
    lse = top + jnp.log(jnp.sum(jnp.exp(scores - top), axis=-1, keepdims=True))
    probs = jnp.exp(scores - lse).astype(jnp.bfloat16)
    attended = jnp.einsum(
        "shqk,skhd->sqhd", probs, grouped(value), preferred_element_type=jnp.float32
    )
    return (attended.reshape(tokens, heads, HD), lse[..., 0])


def attention_backward(query, key, value, lse, d_att, attended):
    tokens, heads = (query.shape[0], query.shape[1])
    delta = jnp.sum(d_att.astype(jnp.float32) * attended.astype(jnp.float32), axis=-1)
    delta = jnp.swapaxes(grouped(delta), 1, 2)
    query_s, key_s, value_s, grads_s = (
        grouped(query),
        grouped(key),
        grouped(value),
        grouped(d_att),
    )
    probs = jnp.exp(masked_scores(query_s, key_s) - lse[..., None])
    d_probs = jnp.einsum("sqhd,skhd->shqk", grads_s, value_s, preferred_element_type=jnp.float32)
    d_scores = (probs * (d_probs - delta[..., None])).astype(jnp.bfloat16)
    d_query = jnp.einsum("shqk,skhd->sqhd", d_scores, key_s, preferred_element_type=jnp.float32)
    d_key = jnp.einsum("shqk,sqhd->skhd", d_scores, query_s, preferred_element_type=jnp.float32)
    d_value = jnp.einsum(
        "shqk,sqhd->skhd", probs.astype(jnp.bfloat16), grads_s, preferred_element_type=jnp.float32
    )
    shape = (tokens, heads, HD)
    return (d_query.reshape(shape), d_key.reshape(shape), d_value.reshape(shape))


def layer_forward(u, params):
    gains, biases, wqkv, wout, wup, wdown = params
    tokens, width = u.shape
    local = wqkv.shape[2]
    heads = local // HD
    normed, rstd = normalize(u)
    gain = gains.astype(jnp.float32)
    bias = biases.astype(jnp.float32)
    first = (normed * gain[0] + bias[0]).astype(jnp.bfloat16)
    second = (normed * gain[1] + bias[1]).astype(jnp.bfloat16)
    qkv = jnp.dot(
        first, wqkv.reshape(width, 3 * local), preferred_element_type=jnp.float32
    ).reshape(tokens, 3, heads, HD)
    qpos = jnp.arange(tokens, dtype=jnp.int32) % SEQ
    cosine, sine = angles(qpos, HD)
    query = (rotate(qkv[:, 0], cosine, sine) * HD ** (-0.5)).astype(jnp.bfloat16)
    key = rotate(qkv[:, 1], cosine, sine).astype(jnp.bfloat16)
    value = qkv[:, 2].astype(jnp.bfloat16)
    attended, lse = attention_forward(query, key, value)
    attended = attended.astype(jnp.bfloat16).reshape(tokens, local)
    hidden = jnp.dot(second, wup, preferred_element_type=jnp.float32)
    act = jax.nn.gelu(hidden, approximate=False).astype(jnp.bfloat16)
    branch = jnp.dot(attended, wout, preferred_element_type=jnp.float32) + jnp.dot(
        act, wdown, preferred_element_type=jnp.float32
    )
    total = lax.psum(branch, "tensor")
    result = (u.astype(jnp.float32) + total).astype(jnp.bfloat16)
    return (result, (normed, rstd, first, second, query, key, value, attended, lse, hidden, act))


def layer_backward(grad, saved, params):
    normed, rstd, first, second, query, key, value, attended, lse, hidden, act = saved
    gains, biases, wqkv, wout, wup, wdown = params
    tokens, width = grad.shape
    local = wqkv.shape[2]
    heads = local // HD
    grad_half = grad.astype(jnp.bfloat16)
    d_down = jnp.dot(act.T, grad_half, preferred_element_type=jnp.float32)
    d_act = jnp.dot(grad_half, wdown.T, preferred_element_type=jnp.float32)
    d_hidden = (d_act * gelu_slope(hidden)).astype(jnp.bfloat16)
    d_up = jnp.dot(second.T, d_hidden, preferred_element_type=jnp.float32)
    d_second = jnp.dot(d_hidden, wup.T, preferred_element_type=jnp.float32)
    d_wout = jnp.dot(attended.T, grad_half, preferred_element_type=jnp.float32)
    d_att = (
        jnp.dot(grad_half, wout.T, preferred_element_type=jnp.float32)
        .astype(jnp.bfloat16)
        .reshape(tokens, heads, HD)
    )
    d_query, d_key, d_value = attention_backward(
        query, key, value, lse, d_att, attended.reshape(tokens, heads, HD)
    )
    qpos = jnp.arange(tokens, dtype=jnp.int32) % SEQ
    cosine, sine = angles(qpos, HD)
    dq_back = rotate(d_query * HD ** (-0.5), cosine, -sine)
    dk_back = rotate(d_key, cosine, -sine)
    d_qkv = (
        jnp.stack([dq_back, dk_back, d_value], axis=1)
        .astype(jnp.bfloat16)
        .reshape(tokens, 3 * local)
    )
    d_wqkv = jnp.dot(first.T, d_qkv, preferred_element_type=jnp.float32).reshape(width, 3, local)
    d_first = jnp.dot(d_qkv, wqkv.reshape(width, 3 * local).T, preferred_element_type=jnp.float32)
    d_first, d_second = lax.psum((d_first, d_second), "tensor")
    gain = gains.astype(jnp.float32)
    d_gains = jnp.stack([jnp.sum(d_first * normed, axis=0), jnp.sum(d_second * normed, axis=0)])
    d_biases = jnp.stack([jnp.sum(d_first, axis=0), jnp.sum(d_second, axis=0)])
    d_norm = d_first * gain[0] + d_second * gain[1]
    d_input = grad + rstd * (
        d_norm
        - jnp.mean(d_norm, axis=-1, keepdims=True)
        - normed * jnp.mean(d_norm * normed, axis=-1, keepdims=True)
    )
    return (d_input, (d_gains, d_biases, d_wqkv, d_wout, d_up, d_down))


def shards(inputs, cotangent, norm_gains, norm_biases, w_qkv, w_out, w_up, w_down):
    section = lax.axis_index("section")
    micro = inputs.shape[0]
    gathered = (
        lax.all_gather(norm_gains, "fsdp", axis=2, tiled=True),
        lax.all_gather(norm_biases, "fsdp", axis=2, tiled=True),
        lax.all_gather(w_qkv, "fsdp", axis=1, tiled=True),
        lax.all_gather(w_out, "fsdp", axis=2, tiled=True),
        lax.all_gather(w_up, "fsdp", axis=1, tiled=True),
        lax.all_gather(w_down, "fsdp", axis=2, tiled=True),
    )
    params = tuple((piece[0] for piece in gathered))
    received = jnp.zeros(inputs.shape[1:], jnp.bfloat16)
    store = None
    for tick in range(micro + 1):
        index = tick - section
        slot = jnp.clip(index, 0, micro - 1)
        valid = (index >= 0) & (index < micro)
        own = inputs[min(tick, micro - 1)]
        entering = jnp.where(section == 0, own, received)
        result, saved = layer_forward(entering, params)
        record = (result,) + saved
        if store is None:
            store = tuple((jnp.stack([item] * micro) for item in record))
        else:
            store = tuple(
                (
                    jnp.where(valid, lax.dynamic_update_index_in_dim(buffer, item, slot, 0), buffer)
                    for buffer, item in zip(store, record)
                )
            )
        if tick < micro:
            received = shifted(result, "section", 1)
    regathered = (
        lax.all_gather(norm_gains, "fsdp", axis=2, tiled=True),
        lax.all_gather(norm_biases, "fsdp", axis=2, tiled=True),
        lax.all_gather(w_qkv, "fsdp", axis=1, tiled=True),
        lax.all_gather(w_out, "fsdp", axis=2, tiled=True),
        lax.all_gather(w_up, "fsdp", axis=1, tiled=True),
        lax.all_gather(w_down, "fsdp", axis=2, tiled=True),
    )
    again = tuple((piece[0] for piece in regathered))
    incoming = jnp.zeros(inputs.shape[1:], jnp.float32)
    totals = None
    grads_in = None
    for tick in range(micro + 1):
        index = tick - 1 + section
        slot = jnp.clip(index, 0, micro - 1)
        valid = (index >= 0) & (index < micro)
        record = tuple(
            (lax.dynamic_index_in_dim(buffer, slot, 0, keepdims=False) for buffer in store)
        )
        grad = lax.dynamic_index_in_dim(cotangent[0], slot, 0, keepdims=False) + jnp.where(
            section == 0, incoming, 0.0
        )
        d_input, pieces = layer_backward(grad, record[1:], again)
        pieces = tuple((jnp.where(valid, piece, 0.0) for piece in pieces))
        if totals is None:
            totals = pieces
            grads_in = jnp.stack([d_input] * micro)
        else:
            totals = tuple((left + right for left, right in zip(totals, pieces)))
        grads_in = jnp.where(
            valid, lax.dynamic_update_index_in_dim(grads_in, d_input, slot, 0), grads_in
        )
        if tick < micro:
            incoming = shifted(d_input, "section", -1)
    gain_total, bias_total, qkv_total, out_total, up_total, down_total = totals
    summed = (
        lax.psum_scatter(gain_total[None], "fsdp", scatter_dimension=2, tiled=True),
        lax.psum_scatter(bias_total[None], "fsdp", scatter_dimension=2, tiled=True),
        lax.psum_scatter(qkv_total[None], "fsdp", scatter_dimension=1, tiled=True),
        lax.psum_scatter(out_total[None], "fsdp", scatter_dimension=2, tiled=True),
        lax.psum_scatter(up_total[None], "fsdp", scatter_dimension=1, tiled=True),
        lax.psum_scatter(down_total[None], "fsdp", scatter_dimension=2, tiled=True),
    )
    return (
        store[0][None],
        grads_in[None],
        summed[0],
        summed[1],
        summed[2],
        summed[3],
        summed[4],
        summed[5],
    )


def solution(mesh):
    in_specs = (
        P(None, "fsdp", None),
        P("section", None, "fsdp", None),
        P("section", None, "fsdp"),
        P("section", None, "fsdp"),
        P("section", "fsdp", None, "tensor"),
        P("section", "tensor", "fsdp"),
        P("section", "fsdp", "tensor"),
        P("section", "tensor", "fsdp"),
    )
    out_specs = (
        P("section", None, "fsdp", None),
        P("section", None, "fsdp", None),
        P("section", None, "fsdp"),
        P("section", None, "fsdp"),
        P("section", "fsdp", None, "tensor"),
        P("section", "tensor", "fsdp"),
        P("section", "fsdp", "tensor"),
        P("section", "tensor", "fsdp"),
    )
    return jax.shard_map(shards, mesh=mesh, in_specs=in_specs, out_specs=out_specs, check_vma=False)
```

profile of v0, /device:TPU:0, one launch (start us, length us, event | category | flops | bytes accessed | tf_op | source)
XLA Modules:
  0.0 1191.5 jit_solution(10730510585829965908)
XLA Ops:
  11.3 22.5 %all_gather.24 = bf16[1,2,1024]{2,1,0:T(2,128)(2,1)S(1)} all-gather(bf16[1,2,128]{2,1,0:T(2,128)(2,1)} %param.11), channel_id=1, replica_groups=mesh['section'=2,'fsdp'=8,'tensor'=2] {'fsdp'}, dimensions={2}, use_global_device_ids=true | all-gather | bytes 4608 | tf_op jit(solution)/shard_map/all_gather | solution.py:175
  33.7 16.7 %all_gather.23 = bf16[1,2,1024]{2,1,0:T(2,128)(2,1)S(1)} all-gather(bf16[1,2,128]{2,1,0:T(2,128)(2,1)} %param.10), channel_id=1, replica_groups=mesh['section'=2,'fsdp'=8,'tensor'=2] {'fsdp'}, dimensions={2}, use_global_device_ids=true | all-gather | bytes 4608 | tf_op jit(solution)/shard_map/all_gather | solution.py:174
  60.8 55.7 %all-gather.5.cloned.1.call-done = bf16[1,1024,3,512]{1,3,2,0:T(8,128)(2,1)} async-done(((bf16[1,128,3,512]{1,3,2,0:T(8,128)(2,1)}), bf16[1,1024,3,512]{1,3,2,0:T(8,128)(2,1)}) %all-gather.5.cloned.1.call-update) | async-done | bytes 3145744 | tf_op jit(solution)/shard_map/all_gather | solution.py:176
  116.5 2.9 fusion.217
  121.7 67.9 %all-gather.9.cloned.1.call-done = bf16[1,1024,2048]{2,1,0:T(8,128)(2,1)} async-done(((bf16[1,128,2048]{2,1,0:T(8,128)(2,1)}), bf16[1,1024,2048]{2,1,0:T(8,128)(2,1)}) %all-gather.9.cloned.1.call-update) | async-done | bytes 4194320 | tf_op jit(solution)/shard_map/all_gather | solution.py:178
  189.6 5.9 fusion.59
  195.5 69.2 %all-gather.11.cloned.1.call-done = bf16[1,2048,1024]{2,1,0:T(8,128)(2,1)} async-done(((bf16[1,2048,128]{2,1,0:T(8,128)(2,1)}), bf16[1,2048,1024]{2,1,0:T(8,128)(2,1)}) %all-gather.11.cloned.1.call-update) | async-done | bytes 4194320 | tf_op jit(solution)/shard_map/all_gather | solution.py:179
  264.7 2.9 fusion.10
  270.9 3.2 pad_maximum_fusion
  274.1 21.7 %all-reduce.9.cloned.1.call-done = f32[128,1024]{1,0:T(8,128)} async-done(((f32[128,1024]{1,0:T(8,128)}), f32[128,1024]{1,0:T(8,128)}) %all-reduce.9.cloned.1.call-update) | async-done | bytes 524304 | tf_op jit(solution)/shard_map/psum | solution.py:120
  306.3 4.9 fusion.152
  315.7 2.8 fusion.80
  318.5 24.3 %all-reduce.11.cloned.1.call-done = f32[128,1024]{1,0:T(8,128)} async-done(((f32[128,1024]{1,0:T(8,128)}), f32[128,1024]{1,0:T(8,128)}) %all-reduce.11.cloned.1.call-update) | async-done | bytes 524304 | tf_op jit(solution)/shard_map/psum | solution.py:120
  342.8 2.7 fusion.192
  357.8 3.9 fusion.162
  366.0 2.6 fusion.39
  376.7 35.3 %all-reduce.17.cloned.1.call-done = (f32[128,1024]{1,0:T(8,128)}, f32[128,1024]{1,0:T(8,128)}) async-done(((f32[128,1024]{1,0:T(8,128)}, f32[128,1024]{1,0:T(8,128)}), (f32[128,1024]{1,0:T(8,128)}, f32[128,1024]{1,0:T(8,128)})) %all-reduce.17.cloned.1.call-update) | async-done | bytes 1048592 | tf_op jit(solution)/shard_map/psum | solution.py:157
  437.4 2.3 pad_maximum_fusion.2
  441.9 35.7 %all-reduce.15.cloned.1.call-done = (f32[128,1024]{1,0:T(8,128)}, f32[128,1024]{1,0:T(8,128)}) async-done(((f32[128,1024]{1,0:T(8,128)}, f32[128,1024]{1,0:T(8,128)}), (f32[128,1024]{1,0:T(8,128)}, f32[128,1024]{1,0:T(8,128)})) %all-reduce.15.cloned.1.call-update) | async-done | bytes 1048592 | tf_op jit(solution)/shard_map/psum | solution.py:157
  479.3 2.8 fusion.169
  508.2 48.9 %all-reduce.13.cloned.1.call-done = (f32[128,1024]{1,0:T(8,128)}, f32[128,1024]{1,0:T(8,128)}, f32[128,1024]{1,0:T(8,128)}) async-done(((f32[128,1024]{1,0:T(8,128)}, f32[128,1024]{1,0:T(8,128)}, f32[128,1024]{1,0:T(8,128)}), (f32[128,1024]{1,0:T(8,128)}, f32[128,1024]{1,0:T(8,128)}, f32[128,1024]{1,0:T(8,128)})) %all-reduce.13.cloned.1.call-update) | async-done | bytes 1572880 | tf_op jit(solution)/shard_map/psum | solution.py:120
  557.1 3.4 fusion.167
  563.0 3.6 add_bitcast_fusion.3
  571.0 4.0 add_bitcast_fusion.2
  578.7 5.3 add_bitcast_fusion.1
  587.8 5.3 add_bitcast_fusion
  600.6 23.8 %reduce-scatter.19.cloned.1.call-done = f32[128,2]{1,0:T(8,128)} async-done(((f32[1024,2]{1,0:T(8,128)}), f32[128,2]{1,0:T(8,128)}) %reduce-scatter.19.cloned.1.call-update) | async-done | bytes 1040
  625.8 63.5 %reduce-scatter.21.cloned.1.call-done = f32[128,2]{1,0:T(8,128)} async-done(((f32[1024,2]{1,0:T(8,128)}), f32[128,2]{1,0:T(8,128)}) %reduce-scatter.21.cloned.1.call-update) | async-done | bytes 1040
  690.9 70.4 %reduce-scatter.13.cloned.1.call-done = f32[1,512,128]{2,1,0:T(8,128)} async-done(((f32[1,512,1024]{2,1,0:T(8,128)}), f32[1,512,128]{2,1,0:T(8,128)}) %reduce-scatter.13.cloned.1.call-update) | async-done | bytes 262160 | tf_op jit(solution)/shard_map/reduce_scatter | solution.py:242
  761.2 121.7 %reduce-scatter.11.cloned.1.call-done = f32[1,128,3,512]{3,1,2,0:T(8,128)} async-done(((f32[1,1024,3,512]{3,1,2,0:T(8,128)}), f32[1,128,3,512]{3,1,2,0:T(8,128)}) %reduce-scatter.11.cloned.1.call-update) | async-done | bytes 786448 | tf_op jit(solution)/shard_map/reduce_scatter | solution.py:241
  882.9 150.8 %reduce-scatter.15.cloned.1.call-done = f32[1,128,2048]{2,1,0:T(8,128)} async-done(((f32[1,1024,2048]{2,1,0:T(8,128)}), f32[1,128,2048]{2,1,0:T(8,128)}) %reduce-scatter.15.cloned.1.call-update) | async-done | bytes 1048592 | tf_op jit(solution)/shard_map/reduce_scatter | solution.py:243
  1033.7 151.1 %reduce-scatter.17.cloned.1.call-done = f32[1,2048,128]{2,1,0:T(8,128)} async-done(((f32[1,2048,1024]{2,1,0:T(8,128)}), f32[1,2048,128]{2,1,0:T(8,128)}) %reduce-scatter.17.cloned.1.call-update) | async-done | bytes 1048592 | tf_op jit(solution)/shard_map/reduce_scatter | solution.py:244
  (452 shorter events, 137.9 us)
Async XLA Ops:
  7.2 51.0 %all-gather.7.cloned.1.call-start = ((), (), s32[]{:S(2)}) async-start(), calls=%async_computation.7 | async-start | bytes 1179648 | tf_op jit(solution)/shard_map/all_gather | solution.py:177
  7.9 108.6 %all-gather.5.cloned.1.call-start = ((), (), s32[]{:S(2)}) async-start(), calls=%async_computation.6 | async-start | bytes 3538944 | tf_op jit(solution)/shard_map/all_gather | solution.py:176
  9.9 179.7 %all-gather.9.cloned.1.call-start = ((), (), s32[]{:S(2)}) async-start(), calls=%async_computation.8 | async-start | bytes 4718592 | tf_op jit(solution)/shard_map/all_gather | solution.py:178
  10.6 254.1 %all-gather.11.cloned.1.call-start = ((), (), s32[]{:S(2)}) async-start(), calls=%async_computation.9 | async-start | bytes 4718592 | tf_op jit(solution)/shard_map/all_gather | solution.py:179
  11.2 284.6 %all-reduce.9.cloned.1.call-start = ((), (), s32[]{:S(2)}) async-start(), calls=%async_computation.10 | async-start | bytes 1048576 | tf_op jit(solution)/shard_map/psum | solution.py:120
  50.5 70.6 %copy-start.84 = (pred[128,128]{0,1:T(8,128)(4,1)}, pred[128,128]{0,1:T(8,128)(4,1)S(1)}, u32[]{:S(2)}) copy-start(pred[128,128]{0,1:T(8,128)(4,1)S(1)} %iota_compare_fusion) | copy-start | bytes 49156
  54.5 64.9 %copy-start.42 = (bf16[1,128,1024]{2,1,0:T(8,128)(2,1)}, bf16[1,128,1024]{2,1,0:T(8,128)(2,1)S(1)}, u32[]{:S(2)}) copy-start(bf16[1,128,1024]{2,1,0:T(8,128)(2,1)S(1)} %get-tuple-element.59) | copy-start | bytes 786436
  54.5 135.1 %copy-start.56 = (bf16[1,128,1024]{2,1,0:T(8,128)(2,1)}, bf16[1,128,1024]{2,1,0:T(8,128)(2,1)S(1)}, u32[]{:S(2)}) copy-start(bf16[1,128,1024]{2,1,0:T(8,128)(2,1)S(1)} %get-tuple-element.60) | copy-start | bytes 786436
  58.1 61.3 %copy-start.103 = (f32[128,8]{0,1:T(8,128)}, f32[128,8]{0,1:T(8,128)S(1)}, u32[]{:S(2)}) copy-start(f32[128,8]{0,1:T(8,128)S(1)} %get-tuple-element.123) | copy-start | bytes 12292
  121.5 147.3 %copy-start.98 = (f32[8,128]{1,0:T(8,128)}, f32[8,128]{1,0:T(8,128)S(1)}, u32[]{:S(2)}) copy-start(f32[8,128]{1,0:T(8,128)S(1)} %log_add_fusion.2) | copy-start | bytes 12292
  195.5 73.9 %copy-start.62 = (bf16[128,2048]{1,0:T(8,128)(2,1)}, bf16[128,2048]{1,0:T(8,128)(2,1)S(1)}, u32[]{:S(2)}) copy-start(bf16[128,2048]{1,0:T(8,128)(2,1)S(1)} %get-tuple-element.127) | copy-start | bytes 1572868
  195.5 72.1 %copy-start.10 = (bf16[1,512,1024]{2,1,0:T(8,128)(2,1)S(1)}, bf16[1,512,1024]{2,1,0:T(8,128)(2,1)}, u32[]{:S(2)}) copy-start(bf16[1,512,1024]{2,1,0:T(8,128)(2,1)} %all-gather.7.cloned.1.call-done) | copy-start | bytes 3145732
  268.8 74.0 %all-reduce.11.cloned.1.call-start = ((), (), s32[]{:S(2)}) async-start(), calls=%async_computation.11 | async-start | bytes 1048576 | tf_op jit(solution)/shard_map/psum | solution.py:120
  297.0 4.0 collective-permute-start
  302.0 40.8 %copy-start.18 = (bf16[128,1024]{1,0:T(8,128)(2,1)}, bf16[128,1024]{1,0:T(8,128)(2,1)S(1)}, u32[]{:S(2)}) copy-start(bf16[128,1024]{1,0:T(8,128)(2,1)S(1)} %get-tuple-element.51) | copy-start | bytes 786436
  314.0 98.0 %all-reduce.17.cloned.1.call-start = ((), (), s32[]{:S(2)}) async-start(), calls=%async_computation.20 | async-start | bytes 2097152 | tf_op jit(solution)/shard_map/psum | solution.py:157
  345.5 5.6 collective-permute-start.1
  371.8 45.1 %copy-start.87 = (pred[128,128]{0,1:T(8,128)(4,1)S(1)}, pred[128,128]{0,1:T(8,128)(4,1)}, u32[]{:S(2)}) copy-start(pred[128,128]{0,1:T(8,128)(4,1)} %copy-done.84) | copy-start | bytes 49156
  371.8 45.1 %copy-start.107 = (f32[8,128]{1,0:T(8,128)S(1)}, f32[8,128]{1,0:T(8,128)}, u32[]{:S(2)}) copy-start(f32[8,128]{1,0:T(8,128)} %get-tuple-element.103) | copy-start | bytes 12292
  371.8 105.8 %all-reduce.15.cloned.1.call-start = ((), (), s32[]{:S(2)}) async-start(), calls=%async_computation.19 | async-start | bytes 2097152 | tf_op jit(solution)/shard_map/psum | solution.py:157
  415.2 3.8 collective-permute-start.2
  437.3 42.0 %copy-start.121 = (f32[128]{0:T(128)S(1)}, f32[128]{0:T(128)}, u32[]{:S(2)}) copy-start(f32[128]{0:T(128)} %get-tuple-element.120) | copy-start | bytes 1540
  437.3 119.8 %all-reduce.13.cloned.1.call-start = ((), (), s32[]{:S(2)}) async-start(), calls=%async_computation.18 | async-start | bytes 3145728 | tf_op jit(solution)/shard_map/psum | solution.py:120
  482.1 4.4 collective-permute-start.3
  504.6 52.6 %copy-start.14 = (f32[2,128,1024]{2,1,0:T(8,128)S(1)}, f32[2,128,1024]{2,1,0:T(8,128)}, u32[]{:S(2)}) copy-start(f32[2,128,1024]{2,1,0:T(8,128)} %fusion.135) | copy-start | bytes 3145732
  504.6 119.8 %reduce-scatter.19.cloned.1.call-start = ((), (), s32[]{:S(2)}) async-start(), calls=%async_computation.16 | async-start | bytes 589824
  508.2 54.8 %copy-start.77 = (bf16[1,128,512]{1,2,0:T(8,128)(2,1)S(1)}, bf16[1,128,512]{1,2,0:T(8,128)(2,1)}, u32[]{:S(2)}) copy-start(bf16[1,128,512]{1,2,0:T(8,128)(2,1)} %get-tuple-element.91) | copy-start | bytes 393220
  561.6 127.8 %reduce-scatter.21.cloned.1.call-start = ((), (), s32[]{:S(2)}) async-start(), calls=%async_computation.17 | async-start | bytes 589824
  562.8 198.4 %reduce-scatter.13.cloned.1.call-start = ((), (), s32[]{:S(2)}) async-start(), calls=%async_computation.13 | async-start | bytes 2359296 | tf_op jit(solution)/shard_map/reduce_scatter | solution.py:242
  566.7 316.2 %reduce-scatter.11.cloned.1.call-start = ((), (), s32[]{:S(2)}) async-start(), calls=%async_computation.12 | async-start | bytes 7077888 | tf_op jit(solution)/shard_map/reduce_scatter | solution.py:241
  575.1 458.6 %reduce-scatter.15.cloned.1.call-start = ((), (), s32[]{:S(2)}) async-start(), calls=%async_computation.14 | async-start | bytes 9437184 | tf_op jit(solution)/shard_map/reduce_scatter | solution.py:243
  584.0 600.7 %reduce-scatter.17.cloned.1.call-start = ((), (), s32[]{:S(2)}) async-start(), calls=%async_computation.15 | async-start | bytes 9437184 | tf_op jit(solution)/shard_map/reduce_scatter | solution.py:244
  (112 other events, 443.8 us)
Sparse Core Ops, SparseCore 0:
  10.0 42.1 all-gather.6
  54.8 61.6 all-gather.4
  118.6 70.9 all-gather.8
  191.5 73.1 all-gather.10
  268.9 26.8 all-reduce.8
  314.1 28.6 all-reduce.10
  371.9 40.0 all-reduce.16
  437.4 40.0 all-reduce.14
  504.7 52.3 all-reduce.12
  561.7 62.5 reduce-scatter.18
  627.7 61.6 reduce-scatter.20
  693.3 67.8 reduce-scatter.12
  765.4 117.4 reduce-scatter.10
  886.9 146.7 reduce-scatter.14
  1037.7 146.9 reduce-scatter.16
where the time goes:
time: 1200 us; the launch traced here: 1190 us
  waiting for transfers between devices  943 us (79%)
  matrix products  95.1 us (8%)
  other arithmetic  59.2 us (5%)
  blocking collectives  39.2 us (3%)
  local copies, waits for them, and re-layouts  31.2 us (3%)
  between operations  16.1 us (1%)
    reduce_scatter x1, waiting for transfers between devices, shards(): lax.psum_scatter(down_total[None], 'fsdp', scatter_dimension=2, tiled=True)  151 us
    reduce_scatter x1, waiting for transfers between devices, shards(): lax.psum_scatter(up_total[None], 'fsdp', scatter_dimension=1, tiled=True)  151 us
    reduce_scatter x1, waiting for transfers between devices, shards(): lax.psum_scatter(qkv_total[None], 'fsdp', scatter_dimension=1, tiled=True)  122 us
    psum x3, waiting for transfers between devices, layer_forward(): total = lax.psum(branch, 'tensor')  94.9 us
    unnamed x17, waiting for transfers between devices  89.4 us
    psum x2, waiting for transfers between devices, layer_backward(): d_first, d_second = lax.psum((d_first, d_second), 'tensor')  71 us
    reduce_scatter x1, waiting for transfers between devices, shards(): lax.psum_scatter(out_total[None], 'fsdp', scatter_dimension=2, tiled=True)  70.4 us
    all_gather x1, waiting for transfers between devices, shards(): lax.all_gather(w_down, 'fsdp', axis=2, tiled=True)  69.2 us
  transfers between devices with their start and end apart: 19, of which 15 were waited for; matrix products, arithmetic and copies ran while one was open for 8% of the time, Pallas kernels for 0%

commit v1 on v0

--- a/solution.py
+++ b/solution.py
@@ -7,6 +7,11 @@
 HD = 64
 SEQ = 128
 EPS = 1e-05
+
+
+def gather_from_all(x, axis, dim):
+    copies = jnp.concatenate([x] * lax.axis_size(axis), axis=dim)
+    return lax.all_to_all(copies, axis, dim, dim, tiled=True)
 
 
 def shifted(x, axis, by):
@@ -176,7 +181,7 @@
         lax.all_gather(w_qkv, "fsdp", axis=1, tiled=True),
         lax.all_gather(w_out, "fsdp", axis=2, tiled=True),
         lax.all_gather(w_up, "fsdp", axis=1, tiled=True),
-        lax.all_gather(w_down, "fsdp", axis=2, tiled=True),
+        gather_from_all(w_down, "fsdp", 2),
     )
     params = tuple((piece[0] for piece in gathered))
     received = jnp.zeros(inputs.shape[1:], jnp.bfloat16)

time: 1200 us -> 1290 us (1.075)
  waiting for transfers between devices: 943 us -> 782 us
  blocking collectives: 39.2 us -> 170 us
  local copies, waits for them, and re-layouts: 31.2 us -> 104 us
  other arithmetic: 59.2 us -> 89.2 us
    all_gather x1, blocking collectives: 22.5 us -> 109 us  [shards(): lax.all_gather(norm_biases, 'fsdp', axis=2, tiled=True)]
    all_gather x1, waiting for transfers between devices: 67.9 us -> 0.01 us  [shards(): lax.all_gather(w_up, 'fsdp', axis=1, tiled=True)]
    all_gather x1, waiting for transfers between devices: 55.7 us -> 0.01 us  [shards(): lax.all_gather(w_qkv, 'fsdp', axis=1, tiled=True)]
    all_gather x1, blocking collectives: 16.7 us -> 60.5 us  [shards(): lax.all_gather(norm_gains, 'fsdp', axis=2, tiled=True)]
    unnamed x0 -> x1, other arithmetic: none -> 26.7 us
    unnamed x257 -> x277, local copies, waits for them, and re-layouts: 24.8 us -> 50.7 us
    concatenate x0 -> x2, local copies, waits for them, and re-layouts: none -> 21.5 us  [gather_from_all(): copies = jnp.concatenate([x] * lax.axis_size(axis), axis=dim)]
    all_to_all x0 -> x1, local copies, waits for them, and re-layouts: none -> 20 us  [gather_from_all(): return lax.all_to_all(copies, axis, dim, dim, tiled=True)]
  transfers between devices with their start and end apart: 19 -> 20, of which waited for: 15 -> 13; matrix products, arithmetic and copies ran while one was open for 8% -> 17% of each run, Pallas kernels for 0% -> 0%
where the time goes in v1:
time: 1290 us; the launch traced here: 1280 us
  waiting for transfers between devices  782 us (61%)
  blocking collectives  170 us (13%)
  local copies, waits for them, and re-layouts  104 us (8%)
  matrix products  99.6 us (8%)
  other arithmetic  89.2 us (7%)
  between operations  16 us (1%)
  starting transfers between devices  15.2 us (1%)
    reduce_scatter x1, waiting for transfers between devices, shards(): lax.psum_scatter(down_total[None], 'fsdp', scatter_dimension=2, tiled=True)  151 us
    reduce_scatter x1, waiting for transfers between devices, shards(): lax.psum_scatter(up_total[None], 'fsdp', scatter_dimension=1, tiled=True)  151 us
    reduce_scatter x1, waiting for transfers between devices, shards(): lax.psum_scatter(qkv_total[None], 'fsdp', scatter_dimension=1, tiled=True)  122 us
    all_gather x1, blocking collectives, shards(): lax.all_gather(norm_biases, 'fsdp', axis=2, tiled=True)  109 us
    unnamed x17, waiting for transfers between devices  89.3 us
    psum x3, waiting for transfers between devices, layer_forward(): total = lax.psum(branch, 'tensor')  79.3 us
    reduce_scatter x1, waiting for transfers between devices, shards(): lax.psum_scatter(out_total[None], 'fsdp', scatter_dimension=2, tiled=True)  70.4 us
    psum x2, waiting for transfers between devices, layer_backward(): d_first, d_second = lax.psum((d_first, d_second), 'tensor')  68.9 us
  transfers between devices with their start and end apart: 20, of which 13 were waited for; matrix products, arithmetic and copies ran while one was open for 17% of the time, Pallas kernels for 0%

profile of v1, /device:TPU:0, one launch (start us, length us, event | category | flops | bytes accessed | tf_op | source)
XLA Modules:
  0.0 1276.5 jit_solution(9383293950246879591)
XLA Ops:
  20.1 20.7 %copy.137 = bf16[1,2048,1024]{1,0,2:T(2,128)(2,1)} copy(bf16[1,2048,1024]{2,1,0:T(8,128)(2,1)} %constant_dynamic-update-slice_fusion.5) | data formatting | bytes 8388608 | tf_op jit(solution)/shard_map/concatenate | solution.py:13
  41.3 26.7 %reduce.13 = bf16[1024,2048]{1,0:T(8,128)(2,1)} reduce(bf16[1024,1,2048]{2,1,0:T(2,128)(2,1)} %bitcast.651, bf16[]{:T(256)} %broadcast.873), dimensions={1}, to_apply=%bitcast.580.reduce_sub_computation | reduce | bytes 8388610
  68.0 7.9 reshape.1384
  75.9 7.4 all-to-all-start
  84.1 109.3 %all_gather.23 = bf16[1,2,1024]{2,1,0:T(2,128)(2,1)S(1)} all-gather(bf16[1,2,128]{2,1,0:T(2,128)(2,1)S(1)} %copy-done.125), channel_id=1, replica_groups=mesh['section'=2,'fsdp'=8,'tensor'=2] {'fsdp'}, dimensions={2}, use_global_device_ids=true | all-gather | bytes 4608 | tf_op jit(solution)/shard_map/all_gather | solution.py:180
  193.4 60.5 %all_gather.22 = bf16[1,2,1024]{2,1,0:T(2,128)(2,1)S(1)} all-gather(bf16[1,2,128]{2,1,0:T(2,128)(2,1)S(1)} %copy-done.126), channel_id=1, replica_groups=mesh['section'=2,'fsdp'=8,'tensor'=2] {'fsdp'}, dimensions={2}, use_global_device_ids=true | all-gather | bytes 4608 | tf_op jit(solution)/shard_map/all_gather | solution.py:179
  256.5 3.1 fusion.217
  261.3 8.8 reshape.1385
  270.2 20.0 %copy.138 = bf16[1,2048,1024]{2,1,0:T(8,128)(2,1)} copy(bf16[1,2048,1024]{1,0,2:T(2,128)(2,1)} %bitcast.652) | data formatting | bytes 8388608 | tf_op jit(solution)/shard_map/all_to_all | solution.py:14
  290.2 6.0 fusion.59
  301.2 26.0 %all-reduce.9.cloned.1.call-done = f32[128,1024]{1,0:T(8,128)} async-done(((f32[128,1024]{1,0:T(8,128)}), f32[128,1024]{1,0:T(8,128)}) %all-reduce.9.cloned.1.call-update) | async-done | bytes 524304 | tf_op jit(solution)/shard_map/psum | solution.py:125
  336.0 4.9 fusion.152
  361.7 3.1 pad_maximum_fusion
  369.2 4.4 all-reduce.11.cloned.1.call-done
  392.9 3.9 fusion.162
  400.2 49.9 %all-gather.11.cloned.1.call-done = bf16[1,2048,1024]{2,1,0:T(8,128)(2,1)} async-done(((bf16[1,2048,128]{2,1,0:T(8,128)(2,1)}), bf16[1,2048,1024]{2,1,0:T(8,128)(2,1)}) %all-gather.11.cloned.1.call-update) | async-done | bytes 4194320 | tf_op jit(solution)/shard_map/all_gather | solution.py:214
  450.1 4.4 fusion.39
  462.9 33.3 %all-reduce.17.cloned.1.call-done = (f32[128,1024]{1,0:T(8,128)}, f32[128,1024]{1,0:T(8,128)}) async-done(((f32[128,1024]{1,0:T(8,128)}, f32[128,1024]{1,0:T(8,128)}), (f32[128,1024]{1,0:T(8,128)}, f32[128,1024]{1,0:T(8,128)})) %all-reduce.17.cloned.1.call-update) | async-done | bytes 1048592 | tf_op jit(solution)/shard_map/psum | solution.py:162
  516.1 3.0 fusion.36
  526.8 35.6 %all-reduce.15.cloned.1.call-done = (f32[128,1024]{1,0:T(8,128)}, f32[128,1024]{1,0:T(8,128)}) async-done(((f32[128,1024]{1,0:T(8,128)}, f32[128,1024]{1,0:T(8,128)}), (f32[128,1024]{1,0:T(8,128)}, f32[128,1024]{1,0:T(8,128)})) %all-reduce.15.cloned.1.call-update) | async-done | bytes 1048592 | tf_op jit(solution)/shard_map/psum | solution.py:162
  593.4 48.9 %all-reduce.13.cloned.1.call-done = (f32[128,1024]{1,0:T(8,128)}, f32[128,1024]{1,0:T(8,128)}, f32[128,1024]{1,0:T(8,128)}) async-done(((f32[128,1024]{1,0:T(8,128)}, f32[128,1024]{1,0:T(8,128)}, f32[128,1024]{1,0:T(8,128)}), (f32[128,1024]{1,0:T(8,128)}, f32[128,1024]{1,0:T(8,128)}, f32[128,1024]{1,0:T(8,128)})) %all-reduce.13.cloned.1.call-update) | async-done | bytes 1572880 | tf_op jit(solution)/shard_map/psum | solution.py:125
  642.3 3.3 fusion.167
  648.1 3.6 add_bitcast_fusion.3
  656.1 4.0 add_bitcast_fusion.2
  663.8 5.3 add_bitcast_fusion.1
  672.9 5.3 add_bitcast_fusion
  685.7 23.8 %reduce-scatter.19.cloned.1.call-done = f32[128,2]{1,0:T(8,128)} async-done(((f32[1024,2]{1,0:T(8,128)}), f32[128,2]{1,0:T(8,128)}) %reduce-scatter.19.cloned.1.call-update) | async-done | bytes 1040
  710.9 63.5 %reduce-scatter.21.cloned.1.call-done = f32[128,2]{1,0:T(8,128)} async-done(((f32[1024,2]{1,0:T(8,128)}), f32[128,2]{1,0:T(8,128)}) %reduce-scatter.21.cloned.1.call-update) | async-done | bytes 1040
  775.9 70.4 %reduce-scatter.13.cloned.1.call-done = f32[1,512,128]{2,1,0:T(8,128)} async-done(((f32[1,512,1024]{2,1,0:T(8,128)}), f32[1,512,128]{2,1,0:T(8,128)}) %reduce-scatter.13.cloned.1.call-update) | async-done | bytes 262160 | tf_op jit(solution)/shard_map/reduce_scatter | solution.py:247
  846.3 121.7 %reduce-scatter.11.cloned.1.call-done = f32[1,128,3,512]{3,1,2,0:T(8,128)} async-done(((f32[1,1024,3,512]{3,1,2,0:T(8,128)}), f32[1,128,3,512]{3,1,2,0:T(8,128)}) %reduce-scatter.11.cloned.1.call-update) | async-done | bytes 786448 | tf_op jit(solution)/shard_map/reduce_scatter | solution.py:246
  967.9 150.8 %reduce-scatter.15.cloned.1.call-done = f32[1,128,2048]{2,1,0:T(8,128)} async-done(((f32[1,1024,2048]{2,1,0:T(8,128)}), f32[1,128,2048]{2,1,0:T(8,128)}) %reduce-scatter.15.cloned.1.call-update) | async-done | bytes 1048592 | tf_op jit(solution)/shard_map/reduce_scatter | solution.py:248
  1118.8 151.0 %reduce-scatter.17.cloned.1.call-done = f32[1,2048,128]{2,1,0:T(8,128)} async-done(((f32[1,2048,1024]{2,1,0:T(8,128)}), f32[1,2048,128]{2,1,0:T(8,128)}) %reduce-scatter.17.cloned.1.call-update) | async-done | bytes 1048592 | tf_op jit(solution)/shard_map/reduce_scatter | solution.py:249
  (478 shorter events, 170.1 us)
Async XLA Ops:
  7.2 249.3 %all-gather.5.cloned.1.call-start = ((), (), s32[]{:S(2)}) async-start(), calls=%async_computation.7 | async-start | bytes 3538944 | tf_op jit(solution)/shard_map/all_gather | solution.py:181
  9.2 280.9 %all-gather.9.cloned.1.call-start = ((), (), s32[]{:S(2)}) async-start(), calls=%async_computation.9 | async-start | bytes 4718592 | tf_op jit(solution)/shard_map/all_gather | solution.py:183
  75.9 117.5 %copy-start.126 = (bf16[1,2,128]{2,1,0:T(2,128)(2,1)S(1)}, bf16[1,2,128]{2,1,0:T(2,128)(2,1)}, u32[]{:S(2)}) copy-start(bf16[1,2,128]{2,1,0:T(2,128)(2,1)} %param.10) | copy-start | bytes 1540
  75.9 178.0 %copy-start.32 = (bf16[2,128,1024]{2,1,0:T(8,128)(2,1)S(1)}, bf16[2,128,1024]{2,1,0:T(8,128)(2,1)}, u32[]{:S(2)}) copy-start(bf16[2,128,1024]{2,1,0:T(8,128)(2,1)} %param.8) | copy-start | bytes 1572868
  75.9 185.4 %all-to-all-start = ((bf16[8,2,131072]{2,1,0:T(2,128)(2,1)}), bf16[8,2,131072]{2,1,0:T(2,128)(2,1)}, u32[]{:S(2)}, u32[]{:S(2)}) async-start(bf16[8,2,131072]{2,1,0:T(2,128)(2,1)} %reshape.1384), calls=%async_computation | async-start | bytes 8388608 | tf_op jit(solution)/shard_map/all_to_all | solution.py:14
  83.3 215.2 %all-gather.7.cloned.1.call-start = ((), (), s32[]{:S(2)}) async-start(), calls=%async_computation.8 | async-start | bytes 1179648 | tf_op jit(solution)/shard_map/all_gather | solution.py:182
  84.0 243.2 %all-reduce.9.cloned.1.call-start = ((), (), s32[]{:S(2)}) async-start(), calls=%async_computation.10 | async-start | bytes 1048576 | tf_op jit(solution)/shard_map/psum | solution.py:125
  256.5 33.6 %copy-start.53 = (bf16[1,128,1024]{2,1,0:T(8,128)(2,1)}, bf16[1,128,1024]{2,1,0:T(8,128)(2,1)S(1)}, u32[]{:S(2)}) copy-start(bf16[1,128,1024]{2,1,0:T(8,128)(2,1)S(1)} %get-tuple-element.60) | copy-start | bytes 786436
  261.1 69.1 %copy-start.98 = (f32[8,128]{1,0:T(8,128)}, f32[8,128]{1,0:T(8,128)S(1)}, u32[]{:S(2)}) copy-start(f32[8,128]{1,0:T(8,128)S(1)} %log_add_fusion.2) | copy-start | bytes 12292
  298.5 34.8 %copy-start = (bf16[1,1024,3,512]{1,3,2,0:T(8,128)(2,1)S(1)}, bf16[1,1024,3,512]{1,3,2,0:T(8,128)(2,1)}, u32[]{:S(2)}) copy-start(bf16[1,1024,3,512]{1,3,2,0:T(8,128)(2,1)} %all-gather.5.cloned.1.call-done) | copy-start | bytes 9437188
  301.2 72.4 %all-reduce.11.cloned.1.call-start = ((), (), s32[]{:S(2)}) async-start(), calls=%async_computation.11 | async-start | bytes 1048576 | tf_op jit(solution)/shard_map/psum | solution.py:125
  328.4 3.3 collective-permute-start
  333.1 40.5 %copy-start.17 = (bf16[128,1024]{1,0:T(8,128)(2,1)}, bf16[128,1024]{1,0:T(8,128)(2,1)S(1)}, u32[]{:S(2)}) copy-start(bf16[128,1024]{1,0:T(8,128)(2,1)S(1)} %get-tuple-element.51) | copy-start | bytes 786436
  344.7 105.4 %all-gather.11.cloned.1.call-start = ((), (), s32[]{:S(2)}) async-start(), calls=%async_computation.12 | async-start | bytes 4718592 | tf_op jit(solution)/shard_map/all_gather | solution.py:214
  345.3 150.9 %all-reduce.17.cloned.1.call-start = ((), (), s32[]{:S(2)}) async-start(), calls=%async_computation.21 | async-start | bytes 2097152 | tf_op jit(solution)/shard_map/psum | solution.py:162
  354.3 10.6 copy-start.52
  354.3 13.0 %copy-start.37 = (f32[128,2048]{1,0:T(8,128)S(1)}, f32[128,2048]{1,0:T(8,128)}, u32[]{:S(2)}) copy-start(f32[128,2048]{1,0:T(8,128)} %get-tuple-element.128) | copy-start | bytes 3145732
  354.3 13.0 %copy-start.79 = (f32[128,2048]{1,0:T(8,128)S(1)}, f32[128,2048]{1,0:T(8,128)}, u32[]{:S(2)}) copy-start(f32[128,2048]{1,0:T(8,128)} %get-tuple-element.131) | copy-start | bytes 3145732
  376.2 5.7 collective-permute-start.1
  457.7 104.8 %all-reduce.15.cloned.1.call-start = ((), (), s32[]{:S(2)}) async-start(), calls=%async_computation.20 | async-start | bytes 2097152 | tf_op jit(solution)/shard_map/psum | solution.py:162
  499.3 3.8 collective-permute-start.2
  522.2 42.0 %copy-start.122 = (f32[128]{0:T(128)S(1)}, f32[128]{0:T(128)}, u32[]{:S(2)}) copy-start(f32[128]{0:T(128)} %get-tuple-element.120) | copy-start | bytes 1540
  522.2 120.1 %all-reduce.13.cloned.1.call-start = ((), (), s32[]{:S(2)}) async-start(), calls=%async_computation.19 | async-start | bytes 3145728 | tf_op jit(solution)/shard_map/psum | solution.py:125
  567.0 4.4 collective-permute-start.3
  589.7 52.6 %copy-start.13 = (f32[2,128,1024]{2,1,0:T(8,128)S(1)}, f32[2,128,1024]{2,1,0:T(8,128)}, u32[]{:S(2)}) copy-start(f32[2,128,1024]{2,1,0:T(8,128)} %fusion.135) | copy-start | bytes 3145732
  589.8 119.7 %reduce-scatter.19.cloned.1.call-start = ((), (), s32[]{:S(2)}) async-start(), calls=%async_computation.17 | async-start | bytes 589824
  593.4 54.7 %copy-start.74 = (bf16[1,128,512]{1,2,0:T(8,128)(2,1)S(1)}, bf16[1,128,512]{1,2,0:T(8,128)(2,1)}, u32[]{:S(2)}) copy-start(bf16[1,128,512]{1,2,0:T(8,128)(2,1)} %get-tuple-element.91) | copy-start | bytes 393220
  646.7 127.7 %reduce-scatter.21.cloned.1.call-start = ((), (), s32[]{:S(2)}) async-start(), calls=%async_computation.18 | async-start | bytes 589824
  647.9 198.4 %reduce-scatter.13.cloned.1.call-start = ((), (), s32[]{:S(2)}) async-start(), calls=%async_computation.14 | async-start | bytes 2359296 | tf_op jit(solution)/shard_map/reduce_scatter | solution.py:247
  651.8 316.2 %reduce-scatter.11.cloned.1.call-start = ((), (), s32[]{:S(2)}) async-start(), calls=%async_computation.13 | async-start | bytes 7077888 | tf_op jit(solution)/shard_map/reduce_scatter | solution.py:246
  660.2 458.6 %reduce-scatter.15.cloned.1.call-start = ((), (), s32[]{:S(2)}) async-start(), calls=%async_computation.15 | async-start | bytes 9437184 | tf_op jit(solution)/shard_map/reduce_scatter | solution.py:248
  669.1 600.7 %reduce-scatter.17.cloned.1.call-start = ((), (), s32[]{:S(2)}) async-start(), calls=%async_computation.16 | async-start | bytes 9437184 | tf_op jit(solution)/shard_map/reduce_scatter | solution.py:249
  (118 other events, 499.4 us)
Sparse Core Ops, SparseCore 0:
  10.6 65.3 all-gather.4
  78.1 144.8 all-gather.8
  225.1 37.6 all-gather.6
  301.3 25.8 all-reduce.8
  344.8 28.6 all-reduce.10
  375.4 74.6 all-gather.10
  457.8 38.2 all-reduce.16
  522.3 40.0 all-reduce.14
  589.9 52.3 all-reduce.12
  646.8 62.5 reduce-scatter.18
  712.8 61.5 reduce-scatter.20
  778.4 67.8 reduce-scatter.12
  850.5 117.4 reduce-scatter.10
  972.0 146.7 reduce-scatter.14
  1122.8 146.9 reduce-scatter.16
